TPU v7x, 32 devices: a whole 2x2x4 slice. The times are simulated.
32 devices in a mesh: prow: 4 (over y, core), pcol: 8 (over z, x).
Axes of the slice: x: 2, y: 2, z: 4, core: 2. Of those that a mesh axis runs over, the one named last changes fastest.
Arguments:
- matrix: bfloat16 [4096, 2048], P('prow', 'pcol'), may hold values from -6 to 6
- panel_one: bfloat16 [256, 4096], P('pcol', 'prow'), may hold values from -0.375 to 0.375
- panel_two: bfloat16 [256, 4096], P('pcol', 'prow'), may hold values from -0.375 to 0.375
- pivots_one: int32 [256], replicated, may hold values from 0 to 4095, as said below
- pivots_two: int32 [256], replicated, may hold values from 256 to 4095, as said below
Outputs:
- trailing: bfloat16 [4096, 2048], P('prow', 'pcol')
Inputs may be any that keep to these rules, and one draw needn't show every extreme that they name: Each pivots_one[i] is either i or a logical row from 256 to 4095; no row is named twice; 4095 is always named. Each pivots_two[i] is either 256 + i or a logical row from 512 to 4095; no row is named twice; 4095 is always named.
All inputs are finite; a program needn't handle non-finite values.
Results may differ from a plain program's by a relative error of at most 0.006.
Values may be sent and summed in bfloat16 or wider, within the bound.
A program may use at most 64 MiB of HBM per device.

v0:
```python
import jax
import jax.numpy as jnp
from jax import lax
from jax.sharding import PartitionSpec as P


def spread(block, axis, source):
    block = jnp.where(lax.axis_index(axis) == source, block, jnp.zeros_like(block))
    return lax.psum(block, axis)


def logical_rows(local_rows, row_index, process_rows, width):
    return (local_rows // width * process_rows + row_index) * width + local_rows % width


def stored_place(logical, process_rows, width):
    owner_row = logical // width % process_rows
    local_row = logical // width // process_rows * width + logical % width
    return (owner_row, local_row)


def trade_order(pivots, first_row, total_rows):
    width = pivots.shape[0]
    order_map = jnp.arange(total_rows, dtype=jnp.int32)
    pivot_at = first_row + jnp.arange(width, dtype=jnp.int32)
    order_map = order_map.at[pivots].set(pivot_at)
    return order_map.at[pivot_at].set(pivots)


def swap_local(current, old_block, order_map, logical, first_row, width):
    source = jnp.take(order_map, logical)
    is_moved = (logical >= first_row + width) & (source != logical)
    filled = jnp.take(old_block, jnp.clip(source - first_row, 0, width - 1), axis=0)
    return jnp.where(is_moved[:, None], filled, current)


def unit_inverse(strict):
    extent = strict.shape[0]
    identity = jnp.eye(extent, dtype=jnp.float32)
    result = identity - strict
    powered = strict
    for repeat in range((extent - 1).bit_length() - 1):
        powered = jnp.dot(powered, powered, precision=lax.Precision.HIGHEST)
        result = jnp.dot(result, identity + powered, precision=lax.Precision.HIGHEST)
    return result


def pivot_solve(incoming, diagonal, section_index, process_rows):
    strict = jnp.tril(diagonal.T.astype(jnp.float32), -1)
    solved = jnp.dot(
        unit_inverse(strict), incoming.astype(jnp.float32), precision=lax.Precision.HIGHEST
    ).astype(jnp.bfloat16)
    solved = spread(solved, "prow", section_index % process_rows)
    return solved


def collect(picker, order_map, first_row, section_index, row_index, process_rows, width):
    sources = order_map[first_row : first_row + width]
    owner_row, local_row = stored_place(sources, process_rows, width)
    is_mine = (owner_row == row_index).astype(jnp.float32)[:, None]
    arriving = picker(local_row).astype(jnp.float32) * is_mine
    block_local = section_index // process_rows * width + jnp.arange(width, dtype=jnp.int32)
    holder = (row_index == section_index % process_rows).astype(jnp.float32)
    leaving = picker(block_local).astype(jnp.float32) * holder
    summed = lax.psum(
        jnp.concatenate([arriving, leaving], axis=0).astype(jnp.bfloat16), "prow"
    ).astype(jnp.float32)
    incoming = summed[:width].astype(jnp.bfloat16)
    old_block = summed[width:].astype(jnp.bfloat16)
    return (incoming, old_block)


def finish(swapped, solved, panel_all, logical, first_row, width):
    product = lax.dot_general(
        panel_all, solved, (((0,), (0,)), ((), ())), preferred_element_type=jnp.float32
    )
    updated = (swapped.astype(jnp.float32) - product).astype(jnp.bfloat16)
    pivot_part = jnp.take(solved, jnp.clip(logical - first_row, 0, width - 1), axis=0)
    in_block = (logical >= first_row) & (logical < first_row + width)
    beyond = logical >= first_row + width
    return jnp.where(beyond[:, None], updated, jnp.where(in_block[:, None], pivot_part, swapped))


def on_device(matrix, panel_one, panel_two, pivots_one, pivots_two):
    rows_dev = matrix.shape[0]
    process_rows = lax.axis_size("prow")
    row_index = lax.axis_index("prow")
    width = panel_one.shape[0] * lax.axis_size("pcol")
    total_rows = rows_dev * process_rows
    logical = logical_rows(jnp.arange(rows_dev, dtype=jnp.int32), row_index, process_rows, width)
    start_two = 1 // process_rows * width
    panel_all_one, panel_all_two = (
        lax.all_gather(panel_one, "pcol", axis=0, tiled=True),
        lax.all_gather(panel_two, "pcol", axis=0, tiled=True),
    )
    diagonal_one = panel_all_one[:, 0:width]
    diagonal_two = panel_all_two[:, start_two : start_two + width]
    order_one = trade_order(pivots_one, 0, total_rows)
    order_two = trade_order(pivots_two, width, total_rows)
    incoming_one, old_one = collect(
        lambda local_row: jnp.take(matrix, local_row, axis=0),
        order_one,
        0,
        0,
        row_index,
        process_rows,
        width,
    )
    swapped_one = swap_local(matrix, old_one, order_one, logical, 0, width)
    solved_one = pivot_solve(incoming_one, diagonal_one, 0, process_rows)
    after_one = finish(swapped_one, solved_one, panel_all_one, logical, 0, width)
    incoming_two, old_two = collect(
        lambda local_row: jnp.take(after_one, local_row, axis=0),
        order_two,
        width,
        1,
        row_index,
        process_rows,
        width,
    )
    swapped_two = swap_local(after_one, old_two, order_two, logical, width, width)
    solved_two = pivot_solve(incoming_two, diagonal_two, 1, process_rows)
    return finish(swapped_two, solved_two, panel_all_two, logical, width, width)


def solution(mesh):
    placed = (P("prow", "pcol"), P("pcol", "prow"), P("pcol", "prow"), P(), P())
    return jax.shard_map(
        on_device, mesh=mesh, in_specs=placed, out_specs=P("prow", "pcol"), check_vma=False
    )
```

profile of v0, /device:TPU:0, one launch (start us, length us, event | category | flops | bytes accessed | tf_op | source)
XLA Modules:
  0.0 230.9 jit_solution(7140232656776959476)
XLA Ops:
  7.2 1.4 scatter_fusion.2
  8.7 1.4 scatter_fusion.3
  10.3 1.2 gather_fusion.2
  11.4 1.2 gather_fusion.3
  14.3 33.0 %all_gather.6 = bf16[256,1024]{1,0:T(8,128)(2,1)S(1)} all-gather(bf16[32,1024]{1,0:T(8,128)(2,1)S(1)} %copy-done.3), channel_id=1, replica_groups=mesh['prow'=4,'pcol'=8] {'pcol'}, dimensions={0}, use_global_device_ids=true | all-gather | bytes 589824 | tf_op jit(solution)/shard_map/all_gather | solution.py:93
  48.7 6.2 %gather_fusion.1 = s32[1024]{0:T(1024)S(1)} fusion(s32[4096]{0:T(1024)S(1)} %scatter_fusion.3, s32[1024]{0:T(1024)S(1)} %fusion.43), kind=kCustom, calls=%fused_computation.3.clone | custom fusion | bytes 12288 | tf_op jit(solution)/shard_map/jit(_take)/gather | solution.py:31
  55.7 1.4 scatter_fusion
  57.1 1.4 scatter_fusion.1
  58.6 6.2 %gather_fusion = s32[1024]{0:T(1024)S(1)} fusion(s32[4096]{0:T(1024)S(1)} %scatter_fusion.1, s32[1024]{0:T(1024)S(1)} %fusion.43), kind=kCustom, calls=%fused_computation.clone | custom fusion | bytes 12288 | tf_op jit(solution)/shard_map/jit(_take)/gather | solution.py:31
  64.8 31.5 %all_gather.7 = bf16[256,1024]{1,0:T(8,128)(2,1)S(1)} all-gather(bf16[32,1024]{1,0:T(8,128)(2,1)S(1)} %copy-done.4), channel_id=1, replica_groups=mesh['prow'=4,'pcol'=8] {'pcol'}, dimensions={0}, use_global_device_ids=true | all-gather | bytes 589824 | tf_op jit(solution)/shard_map/all_gather | solution.py:94
  106.7 1.8 fusion.6
  109.8 3.9 %gather_fusion.4 = bf16[1024,256]{1,0:T(8,128)(2,1)S(1)} fusion(bf16[256,256]{1,0:T(8,128)(2,1)S(1)} %slice-done, s32[1024]{0:T(1024)S(1)} %get-tuple-element.23), kind=kCustom, calls=%fused_computation.2.clone | custom fusion | bytes 1052672 | tf_op jit(solution)/shard_map/jit(_take)/gather | solution.py:33
  113.7 1.0 copy.26
  114.7 26.7 %all-reduce.7.cloned.1.call-done = bf16[256,256]{1,0:T(8,128)(2,1)} async-done(((bf16[256,256]{1,0:T(8,128)(2,1)}), bf16[256,256]{1,0:T(8,128)(2,1)}) %all-reduce.7.cloned.1.call-update) | async-done | bytes 131088 | tf_op jit(solution)/shard_map/psum | solution.py:9
  141.4 4.4 %gather_fusion.5 = bf16[1024,256]{1,0:T(8,128)(2,1)S(1)} fusion(bf16[256,256]{1,0:T(8,128)(2,1)} %all-reduce.7.cloned.1.call-done, s32[1024]{0:T(1024)S(1)} %get-tuple-element.22), kind=kCustom, calls=%fused_computation.7.clone | custom fusion | bytes 1052672 | tf_op jit(solution)/shard_map/jit(_take)/gather | solution.py:78
  145.8 1.0 copy.29
  146.8 1.5 fusion.5
  148.5 1.2 gather_fusion.7
  149.7 1.2 gather_fusion.6
  151.9 32.0 %all-reduce.9.cloned.1.call-done = bf16[512,256]{1,0:T(8,128)(2,1)} async-done(((bf16[512,256]{1,0:T(8,128)(2,1)}), bf16[512,256]{1,0:T(8,128)(2,1)}) %all-reduce.9.cloned.1.call-update) | async-done | bytes 262160 | tf_op jit(solution)/shard_map/psum | solution.py:65
  184.0 1.8 fusion.7
  186.8 3.9 %gather_fusion.8 = bf16[1024,256]{1,0:T(8,128)(2,1)S(1)} fusion(bf16[256,256]{1,0:T(8,128)(2,1)S(1)} %slice-done.1, s32[1024]{0:T(1024)S(1)} %get-tuple-element.25), kind=kCustom, calls=%fused_computation.8.clone | custom fusion | bytes 1052672 | tf_op jit(solution)/shard_map/jit(_take)/gather | solution.py:33
  190.9 26.8 %all-reduce.11.cloned.1.call-done = bf16[256,256]{1,0:T(8,128)(2,1)} async-done(((bf16[256,256]{1,0:T(8,128)(2,1)}), bf16[256,256]{1,0:T(8,128)(2,1)}) %all-reduce.11.cloned.1.call-update) | async-done | bytes 131088 | tf_op jit(solution)/shard_map/psum | solution.py:9
  217.7 4.4 %gather_fusion.9 = bf16[1024,256]{1,0:T(8,128)(2,1)S(1)} fusion(bf16[256,256]{1,0:T(8,128)(2,1)} %all-reduce.11.cloned.1.call-done, s32[1024]{0:T(1024)S(1)} %get-tuple-element.24), kind=kCustom, calls=%fused_computation.9.clone | custom fusion | bytes 1052672 | tf_op jit(solution)/shard_map/jit(_take)/gather | solution.py:78
  (97 shorter events, 20.7 us)
Async XLA Ops:
  6.5 100.2 %all-reduce.5.cloned.1.call-start = ((), (), s32[]{:S(2)}) async-start(), calls=%async_computation | async-start | bytes 524288 | tf_op jit(solution)/shard_map/psum | solution.py:65
  6.5 0.7 copy-start.5
  8.7 1.6 copy-start.2
  13.5 0.8 copy-start.3
  13.5 127.9 %all-reduce.7.cloned.1.call-start = ((), (), s32[]{:S(2)}) async-start(), calls=%async_computation.1 | async-start | bytes 262144 | tf_op jit(solution)/shard_map/psum | solution.py:9
  55.0 0.7 copy-start.6
  58.6 6.2 %copy-start.4 = (bf16[32,1024]{1,0:T(8,128)(2,1)S(1)}, bf16[32,1024]{1,0:T(8,128)(2,1)}, u32[]{:S(2)}) copy-start(bf16[32,1024]{1,0:T(8,128)(2,1)} %param.13) | copy-start | bytes 196612
  108.6 75.4 %all-reduce.9.cloned.1.call-start = ((), (), s32[]{:S(2)}) async-start(), calls=%async_computation.2 | async-start | bytes 524288 | tf_op jit(solution)/shard_map/psum | solution.py:65
  108.8 0.9 slice-start
  145.8 1.0 copy-start
  151.8 65.8 %all-reduce.11.cloned.1.call-start = ((), (), s32[]{:S(2)}) async-start(), calls=%async_computation.3 | async-start | bytes 262144 | tf_op jit(solution)/shard_map/psum | solution.py:9
  185.9 0.9 slice-start.1
  222.1 0.9 copy-start.1
Sparse Core Ops, SparseCore 0:
  13.6 34.6 all-reduce.4
  108.7 32.6 all-reduce.6
  152.0 31.9 all-reduce.8
  186.3 31.3 all-reduce.10
where the time goes:
time: 231 us
  waiting for transfers between devices  85.6 us (37%)
  blocking collectives  64.5 us (28%)
  local copies, waits for them, and re-layouts  48 us (21%)
  matrix products  16.7 us (7%)
  between operations  13.7 us (6%)
    psum x2, waiting for transfers between devices, spread(): return lax.psum(block, axis)  53.4 us
    all_gather x1, blocking collectives, on_device(): lax.all_gather(panel_one, 'pcol', axis=0, tiled=True)  33 us
    psum x2, waiting for transfers between devices, collect(): lax.psum(jnp.concatenate([arriving, leaving], axis=0).astype(jnp.bfloat16...  32.1 us
    all_gather x1, blocking collectives, on_device(): lax.all_gather(panel_two, 'pcol', axis=0, tiled=True)  31.5 us
    gather x2, local copies, waits for them, and re-layouts, swap_local(): source = jnp.take(order_map, logical)  12.3 us
    gather x4, local copies, waits for them, and re-layouts, finish(): jnp.take(solved, jnp.clip(logical - first_row, 0, width - 1), axis=0)  9.97 us
    gather x4, local copies, waits for them, and re-layouts, swap_local(): jnp.take(old_block, jnp.clip(source - first_row, 0, width - 1), axis=0)  9.09 us
    dot_general x14, matrix products, unit_inverse(): jnp.dot(result, identity + powered, precision=lax.Precision.HIGHEST)  5.62 us
  transfers between devices with their start and end apart: 4, of which 3 were waited for; matrix products, arithmetic and copies ran while one was open for 16% of the time, Pallas kernels for 0%

commit v1 on v0

--- a/solution.py
+++ b/solution.py
@@ -2,6 +2,14 @@
 import jax.numpy as jnp
 from jax import lax
 from jax.sharding import PartitionSpec as P
+
+
+def load_region(panel, dim_i):
+    panel = jnp.moveaxis(panel, 0, dim_i)
+    current_arr = panel.shape
+    return panel.reshape(
+        *current_arr[:dim_i], current_arr[dim_i] * current_arr[dim_i + 1], *current_arr[dim_i + 2 :]
+    )
 
 
 def spread(block, axis, source):
@@ -89,9 +97,38 @@
     total_rows = rows_dev * process_rows
     logical = logical_rows(jnp.arange(rows_dev, dtype=jnp.int32), row_index, process_rows, width)
     start_two = 1 // process_rows * width
+
+    def work_streams(d_out, frame, axis_tag="pcol"):
+        n_blocks = lax.axis_size(axis_tag)
+        by_rank = []
+        it = 0
+        while it < n_blocks:
+            by_rank.append((it, (it + 1) % n_blocks))
+            it += 1
+        pool = []
+        for m, j in by_rank:
+            pool.append((j, m))
+        passed, e_now = ([], [])
+        no = 0
+        while no < n_blocks - 1:
+            if no % 2 == 0:
+                passed.append(
+                    lax.ppermute(passed[-1] if passed else frame, axis_name=axis_tag, perm=by_rank)
+                )
+            else:
+                e_now.append(
+                    lax.ppermute(e_now[-1] if e_now else frame, axis_name=axis_tag, perm=pool)
+                )
+            no = no + 1
+        raw_out = jnp.stack([*passed[::-1], frame, *e_now])
+        h_now = lax.axis_index(axis_tag)
+        y_new = h_now - len(passed)
+        raw_out = raw_out[(jnp.arange(n_blocks) - y_new) % n_blocks]
+        return load_region(raw_out, d_out)
+
     panel_all_one, panel_all_two = (
         lax.all_gather(panel_one, "pcol", axis=0, tiled=True),
-        lax.all_gather(panel_two, "pcol", axis=0, tiled=True),
+        work_streams(0, panel_two),
     )
     diagonal_one = panel_all_one[:, 0:width]
     diagonal_two = panel_all_two[:, start_two : start_two + width]

time: 231 us -> 206 us (0.89)
  blocking collectives: 64.5 us -> 31.3 us
  waiting for transfers between devices: 85.6 us -> 66.9 us
  starting transfers between devices: 0.35 us -> 17.3 us
  other arithmetic: 2.1 us -> 7.82 us
  local copies, waits for them, and re-layouts: 48 us -> 52.5 us
    all_gather x1 -> x0, blocking collectives: 31.5 us -> none  [on_device(): lax.all_gather(panel_two, 'pcol', axis=0, tiled=True)]
    ppermute x0 -> x7, starting transfers between devices: none -> 17 us  [the longest x3 12.5 us: work_streams(): lax.ppermute(e_now[-1] if e_now else frame, axis_name=axis_tag, perm=pool)]
    psum x2, waiting for transfers between devices: 32.1 us -> 16.8 us  [collect(): lax.psum(jnp.concatenate([arriving, leaving], axis=0).astype(jnp.bfloat16...]
    psum x2, waiting for transfers between devices: 53.4 us -> 45.6 us  [spread(): return lax.psum(block, axis)]
    unnamed x17 -> x58, local copies, waits for them, and re-layouts: 3.2 us -> 8.18 us
    ppermute x0 -> x7, waiting for transfers between devices: none -> 4.49 us  [the longest x4 4.49 us: work_streams(): lax.ppermute(passed[-1] if passed else frame, axis_name=axis_tag, perm=by...]
  transfers between devices with their start and end apart: 4 -> 11, of which waited for: 3 -> 4; matrix products, arithmetic and copies ran while one was open for 16% -> 30% of each run, Pallas kernels for 0% -> 0%
where the time goes in v1:
time: 206 us
  waiting for transfers between devices  66.9 us (32%)
  local copies, waits for them, and re-layouts  52.5 us (25%)
  blocking collectives  31.3 us (15%)
  starting transfers between devices  17.3 us (8%)
  matrix products  16.2 us (8%)
  between operations  13.9 us (7%)
  other arithmetic  7.82 us (4%)
    psum x2, waiting for transfers between devices, spread(): return lax.psum(block, axis)  45.6 us
    all_gather x1, blocking collectives, on_device(): lax.all_gather(panel_one, 'pcol', axis=0, tiled=True)  31.3 us
    psum x2, waiting for transfers between devices, collect(): lax.psum(jnp.concatenate([arriving, leaving], axis=0).astype(jnp.bfloat16...  16.8 us
    ppermute x3, starting transfers between devices, work_streams(): lax.ppermute(e_now[-1] if e_now else frame, axis_name=axis_tag, perm=pool)  12.5 us
    gather x2, local copies, waits for them, and re-layouts, swap_local(): source = jnp.take(order_map, logical)  12.3 us
    gather x4, local copies, waits for them, and re-layouts, finish(): jnp.take(solved, jnp.clip(logical - first_row, 0, width - 1), axis=0)  9.17 us
    gather x4, local copies, waits for them, and re-layouts, swap_local(): jnp.take(old_block, jnp.clip(source - first_row, 0, width - 1), axis=0)  8.28 us
    unnamed x58, local copies, waits for them, and re-layouts  8.18 us
  transfers between devices with their start and end apart: 11, of which 4 were waited for; matrix products, arithmetic and copies ran while one was open for 30% of the time, Pallas kernels for 0%

profile of v1, /device:TPU:0, one launch (start us, length us, event | category | flops | bytes accessed | tf_op | source)
XLA Modules:
  0.0 205.9 jit_solution(1467863529351791671)
XLA Ops:
  6.5 2.9 %collective-permute-start = (bf16[32,1024]{1,0:T(8,128)(2,1)}, bf16[32,1024]{1,0:T(8,128)(2,1)S(1)}, u32[]{:S(2)}, u32[]{:S(2)}) collective-permute-start(bf16[32,1024]{1,0:T(8,128)(2,1)} %param.13), channel_id=1, source_target_pairs={{0,1},{1,2},{2,3},{3,4},{4,5},{5,6},{6,7},{7,0},{8,9},{9,10},{10,1... | collective-permute-start | bytes 196616 | tf_op jit(solution)/shard_map/ppermute | solution.py:116
  9.5 3.0 %collective-permute-start.4 = (bf16[32,1024]{1,0:T(8,128)(2,1)}, bf16[32,1024]{1,0:T(8,128)(2,1)S(1)}, u32[]{:S(2)}, u32[]{:S(2)}) collective-permute-start(bf16[32,1024]{1,0:T(8,128)(2,1)} %param.13), channel_id=1, source_target_pairs={{1,0},{2,1},{3,2},{4,3},{5,4},{6,5},{7,6},{0,7},{9,8},{10,9},{11,1... | collective-permute-start | bytes 196616 | tf_op jit(solution)/shard_map/ppermute | solution.py:120
  13.2 1.4 scatter_fusion.2
  14.7 1.4 scatter_fusion.3
  20.3 31.3 %all_gather.3 = bf16[256,1024]{1,0:T(8,128)(2,1)S(1)} all-gather(bf16[32,1024]{1,0:T(8,128)(2,1)S(1)} %copy-done.3), channel_id=1, replica_groups=mesh['prow'=4,'pcol'=8] {'pcol'}, dimensions={0}, use_global_device_ids=true | all-gather | bytes 589824 | tf_op jit(solution)/shard_map/all_gather | solution.py:130
  53.0 6.2 %gather_fusion.2 = s32[1024]{0:T(1024)S(1)} fusion(s32[4096]{0:T(1024)S(1)} %scatter_fusion.3, s32[1024]{0:T(1024)S(1)} %fusion.42), kind=kCustom, calls=%fused_computation.3.clone | custom fusion | bytes 12288 | tf_op jit(solution)/shard_map/jit(_take)/gather | solution.py:39
  60.5 1.4 scatter_fusion
  61.9 1.6 scatter_fusion.1
  64.1 6.1 %gather_fusion.1 = s32[1024]{0:T(1024)S(1)} fusion(s32[4096]{0:T(1024)S(1)} %scatter_fusion.1, s32[1024]{0:T(1024)S(1)} %fusion.42), kind=kCustom, calls=%fused_computation.clone | custom fusion | bytes 12288 | tf_op jit(solution)/shard_map/jit(_take)/gather | solution.py:39
  79.0 4.7 %collective-permute-start.5 = (bf16[32,1024]{1,0:T(8,128)(2,1)S(1)}, bf16[32,1024]{1,0:T(8,128)(2,1)}, u32[]{:S(2)}, u32[]{:S(2)}) collective-permute-start(bf16[32,1024]{1,0:T(8,128)(2,1)S(1)} %collective-permute-done.4), channel_id=1, source_target_pairs={{1,0},{2,1},{3,2},{4,3},{5,4},{6,5},{7,6},{0,7},{9,8},{10,9},{11,1... | collective-permute-start | bytes 196616 | tf_op jit(solution)/shard_map/ppermute | solution.py:120
  83.7 1.8 fusion.5
  87.1 3.9 %gather_fusion.5 = bf16[1024,256]{1,0:T(8,128)(2,1)S(1)} fusion(bf16[256,256]{1,0:T(8,128)(2,1)S(1)} %slice-done, s32[1024]{0:T(1024)S(1)} %get-tuple-element.19), kind=kCustom, calls=%fused_computation.2.clone | custom fusion | bytes 1052672 | tf_op jit(solution)/shard_map/jit(_take)/gather | solution.py:41
  91.3 4.7 %collective-permute-start.6 = (bf16[32,1024]{1,0:T(8,128)(2,1)}, bf16[32,1024]{1,0:T(8,128)(2,1)S(1)}, u32[]{:S(2)}, u32[]{:S(2)}) collective-permute-start(bf16[32,1024]{1,0:T(8,128)(2,1)} %collective-permute-done.5), channel_id=1, source_target_pairs={{1,0},{2,1},{3,2},{4,3},{5,4},{6,5},{7,6},{0,7},{9,8},{10,9},{11,1... | collective-permute-start | bytes 196616 | tf_op jit(solution)/shard_map/ppermute | solution.py:120
  96.1 18.8 %all-reduce.7.cloned.1.call-done = bf16[256,256]{1,0:T(8,128)(2,1)} async-done(((bf16[256,256]{1,0:T(8,128)(2,1)}), bf16[256,256]{1,0:T(8,128)(2,1)}) %all-reduce.7.cloned.1.call-update) | async-done | bytes 131088 | tf_op jit(solution)/shard_map/psum | solution.py:17
  114.9 4.4 %gather_fusion.6 = bf16[1024,256]{1,0:T(8,128)(2,1)S(1)} fusion(bf16[256,256]{1,0:T(8,128)(2,1)} %all-reduce.7.cloned.1.call-done, s32[1024]{0:T(1024)S(1)} %get-tuple-element.18), kind=kCustom, calls=%fused_computation.7.clone | custom fusion | bytes 1052672 | tf_op jit(solution)/shard_map/jit(_take)/gather | solution.py:86
  121.4 1.3 gather_fusion.8
  122.7 1.3 gather_fusion.7
  125.4 1.5 collective-permute-start.3
  128.0 4.5 %collective-permute-done.3 = bf16[32,1024]{1,0:T(8,128)(2,1)S(1)} collective-permute-done((bf16[32,1024]{1,0:T(8,128)(2,1)S(1)}, bf16[32,1024]{1,0:T(8,128)(2,1)S(1)}, u32[]{:S(2)}, u32[]{:S(2)}) %collective-permute-start.3) | collective-permute-done | bytes 65568 | tf_op jit(solution)/shard_map/ppermute | solution.py:116
  142.1 16.8 %all-reduce.9.cloned.1.call-done = bf16[512,256]{1,0:T(8,128)(2,1)} async-done(((bf16[512,256]{1,0:T(8,128)(2,1)}), bf16[512,256]{1,0:T(8,128)(2,1)}) %all-reduce.9.cloned.1.call-update) | async-done | bytes 262160 | tf_op jit(solution)/shard_map/psum | solution.py:73
  158.9 1.8 fusion.6
  161.7 3.9 %gather_fusion.9 = bf16[1024,256]{1,0:T(8,128)(2,1)S(1)} fusion(bf16[256,256]{1,0:T(8,128)(2,1)S(1)} %slice-done.1, s32[1024]{0:T(1024)S(1)} %copy-done.8), kind=kCustom, calls=%fused_computation.8.clone | custom fusion | bytes 1052672 | tf_op jit(solution)/shard_map/jit(_take)/gather | solution.py:41
  165.9 26.7 %all-reduce.11.cloned.1.call-done = bf16[256,256]{1,0:T(8,128)(2,1)} async-done(((bf16[256,256]{1,0:T(8,128)(2,1)}), bf16[256,256]{1,0:T(8,128)(2,1)}) %all-reduce.11.cloned.1.call-update) | async-done | bytes 131088 | tf_op jit(solution)/shard_map/psum | solution.py:17
  192.6 4.4 %gather_fusion.10 = bf16[1024,256]{1,0:T(8,128)(2,1)S(1)} fusion(bf16[256,256]{1,0:T(8,128)(2,1)} %all-reduce.11.cloned.1.call-done, s32[1024]{0:T(1024)S(1)} %copy-done.7), kind=kCustom, calls=%fused_computation.9.clone | custom fusion | bytes 1052672 | tf_op jit(solution)/shard_map/jit(_take)/gather | solution.py:86
  (155 shorter events, 35.9 us)
Async XLA Ops:
  6.5 77.2 %all-reduce.5.cloned.1.call-start = ((), (), s32[]{:S(2)}) async-start(), calls=%async_computation | async-start | bytes 524288 | tf_op jit(solution)/shard_map/psum | solution.py:73
  6.5 72.4 %collective-permute-start = (bf16[32,1024]{1,0:T(8,128)(2,1)}, bf16[32,1024]{1,0:T(8,128)(2,1)S(1)}, u32[]{:S(2)}, u32[]{:S(2)}) collective-permute-start(bf16[32,1024]{1,0:T(8,128)(2,1)} %param.13), channel_id=1, source_target_pairs={{0,1},{1,2},{2,3},{3,4},{4,5},{5,6},{6,7},{7,0},{8,9},{9,10},{10,1... | collective-permute-start | bytes 196616 | tf_op jit(solution)/shard_map/ppermute | solution.py:116
  9.5 69.5 %collective-permute-start.4 = (bf16[32,1024]{1,0:T(8,128)(2,1)}, bf16[32,1024]{1,0:T(8,128)(2,1)S(1)}, u32[]{:S(2)}, u32[]{:S(2)}) collective-permute-start(bf16[32,1024]{1,0:T(8,128)(2,1)} %param.13), channel_id=1, source_target_pairs={{1,0},{2,1},{3,2},{4,3},{5,4},{6,5},{7,6},{0,7},{9,8},{10,9},{11,1... | collective-permute-start | bytes 196616 | tf_op jit(solution)/shard_map/ppermute | solution.py:120
  12.5 6.0 %copy-start.13 = (pred[256]{0:T(512)(128)(4,1)}, pred[256]{0:T(512)(128)(4,1)S(1)}, u32[]{:S(2)}) copy-start(pred[256]{0:T(512)(128)(4,1)S(1)} %broadcast_compare_fusion.2) | copy-start | bytes 772
  14.7 1.6 copy-start.2
  16.2 1.2 copy-start.9
  19.5 95.4 %all-reduce.7.cloned.1.call-start = ((), (), s32[]{:S(2)}) async-start(), calls=%async_computation.1 | async-start | bytes 262144 | tf_op jit(solution)/shard_map/psum | solution.py:17
  20.3 31.9 %copy-start.5 = (s32[256]{0:T(256)}, s32[256]{0:T(256)S(1)}, u32[]{:S(2)}) copy-start(s32[256]{0:T(256)S(1)} %iota_add_fusion.2) | copy-start | bytes 3076
  79.0 12.3 %collective-permute-start.1 = (bf16[32,1024]{1,0:T(8,128)(2,1)S(1)}, bf16[32,1024]{1,0:T(8,128)(2,1)}, u32[]{:S(2)}, u32[]{:S(2)}) collective-permute-start(bf16[32,1024]{1,0:T(8,128)(2,1)S(1)} %collective-permute-done), channel_id=1, source_target_pairs={{0,1},{1,2},{2,3},{3,4},{4,5},{5,6},{6,7},{7,0},{8,9},{9,10},{10,1... | collective-permute-start | bytes 196616 | tf_op jit(solution)/shard_map/ppermute | solution.py:116
  79.0 12.4 %collective-permute-start.5 = (bf16[32,1024]{1,0:T(8,128)(2,1)S(1)}, bf16[32,1024]{1,0:T(8,128)(2,1)}, u32[]{:S(2)}, u32[]{:S(2)}) collective-permute-start(bf16[32,1024]{1,0:T(8,128)(2,1)S(1)} %collective-permute-done.4), channel_id=1, source_target_pairs={{1,0},{2,1},{3,2},{4,3},{5,4},{6,5},{7,6},{0,7},{9,8},{10,9},{11,1... | collective-permute-start | bytes 196616 | tf_op jit(solution)/shard_map/ppermute | solution.py:120
  85.6 73.3 %all-reduce.9.cloned.1.call-start = ((), (), s32[]{:S(2)}) async-start(), calls=%async_computation.2 | async-start | bytes 524288 | tf_op jit(solution)/shard_map/psum | solution.py:73
  86.2 0.9 slice-start
  91.3 34.1 %collective-permute-start.2 = (bf16[32,1024]{1,0:T(8,128)(2,1)}, bf16[32,1024]{1,0:T(8,128)(2,1)S(1)}, u32[]{:S(2)}, u32[]{:S(2)}) collective-permute-start(bf16[32,1024]{1,0:T(8,128)(2,1)} %collective-permute-done.1), channel_id=1, source_target_pairs={{0,1},{1,2},{2,3},{3,4},{4,5},{5,6},{6,7},{7,0},{8,9},{9,10},{10,1... | collective-permute-start | bytes 196616 | tf_op jit(solution)/shard_map/ppermute | solution.py:116
  91.3 43.7 %collective-permute-start.6 = (bf16[32,1024]{1,0:T(8,128)(2,1)}, bf16[32,1024]{1,0:T(8,128)(2,1)S(1)}, u32[]{:S(2)}, u32[]{:S(2)}) collective-permute-start(bf16[32,1024]{1,0:T(8,128)(2,1)} %collective-permute-done.5), channel_id=1, source_target_pairs={{1,0},{2,1},{3,2},{4,3},{5,4},{6,5},{7,6},{0,7},{9,8},{10,9},{11,1... | collective-permute-start | bytes 196616 | tf_op jit(solution)/shard_map/ppermute | solution.py:120
  119.3 0.9 copy-start
  119.3 0.9 copy-start.19
  125.4 7.0 %collective-permute-start.3 = (bf16[32,1024]{1,0:T(8,128)(2,1)S(1)}, bf16[32,1024]{1,0:T(8,128)(2,1)S(1)}, u32[]{:S(2)}, u32[]{:S(2)}) collective-permute-start(bf16[32,1024]{1,0:T(8,128)(2,1)S(1)} %collective-permute-done.2), channel_id=1, source_target_pairs={{0,1},{1,2},{2,3},{3,4},{4,5},{5,6},{6,7},{7,0},{8,9},{9,10},{10,1... | collective-permute-start | bytes 196616 | tf_op jit(solution)/shard_map/ppermute | solution.py:116
  127.7 64.9 %all-reduce.11.cloned.1.call-start = ((), (), s32[]{:S(2)}) async-start(), calls=%async_computation.3 | async-start | bytes 262144 | tf_op jit(solution)/shard_map/psum | solution.py:17
  158.9 1.9 copy-start.8
  160.8 0.9 slice-start.1
  165.6 27.0 %copy-start.7 = (s32[1024]{0:T(1024)S(1)}, s32[1024]{0:T(1024)}, u32[]{:S(2)}) copy-start(s32[1024]{0:T(1024)} %get-tuple-element.20) | copy-start | bytes 12292
  197.0 0.9 copy-start.1
  197.0 0.9 copy-start.17
  197.0 0.9 copy-start.20
  (13 other events, 9.7 us)
Sparse Core Ops, SparseCore 0:
  19.6 30.7 all-reduce.4
  85.7 29.1 all-reduce.6
  127.8 31.0 all-reduce.8
  161.2 31.3 all-reduce.10
